TPU v7x, 256 devices: a whole 4x4x8 slice. The times are simulated.
256 devices in a mesh: layer: 4 (over x_lo, core), feat: 64 (over x_hi, z, y).
Axes of the slice: x: 4 (x_hi: 2, x_lo: 2; x = x_hi * 2 + x_lo), y: 4, z: 8, core: 2. Of those that a mesh axis runs over, the one named last changes fastest.
Arguments:
- sources: bfloat16 [4, 512, 4096], P('layer', 'feat'), may hold values from -6 to 6
- targets: bfloat16 [4, 512, 4096], P('layer', 'feat'), may hold values from -6 to 6
- enc_weight: bfloat16 [4, 8192, 4096], P('layer', 'feat'), may hold values from -0.09375 to 0.09375
- dec_weight: bfloat16 [4, 4, 8192, 4096], P('layer', None, 'feat'), may hold values from -0.0625 to 0.0625
- active: int32 [4, 8192, 512], P('layer', 'feat'), may hold values 0 or 1
Outputs:
- errors: float32 [4, 512, 4096], P('layer', 'feat')
- grad_dec: bfloat16 [4, 4, 8192, 4096], P('layer', None, 'feat')
- grad_enc: bfloat16 [4, 8192, 4096], P('layer', 'feat')
All inputs are finite; a program needn't handle non-finite values. No bound on the sum of `active` on one device may be relied on, other than what follows from the above.
Results may differ from a plain program's by a relative error of at most 0.0061.
Values may be sent and summed in bfloat16 or wider, within the bound.
No kernel may reach another device: no remote copies, remote signals or barrier semaphores. Data moves between devices by JAX's collectives and lax.ppermute only.
A program may use at most 64 MiB of HBM per device.

v0:
```python
import math
import jax
import jax.numpy as jnp
from jax import lax
from jax.sharding import PartitionSpec as P

TOKENS = 512


def on_device(sources, targets, enc_weight, dec_weight, active):
    per_group = sources.shape[0]
    layer_count = dec_weight.shape[1]
    group_index = lax.axis_index("layer")
    source_full = lax.all_gather(sources, "feat", axis=1, tiled=True)
    pre_acts = jnp.einsum(
        "sfd,std->sft", enc_weight, source_full, preferred_element_type=jnp.float32
    )
    features = (active.astype(jnp.float32) * pre_acts).astype(jnp.bfloat16)
    all_features = lax.all_gather(features, "layer", axis=0, tiled=True)
    target_pos = group_index * per_group + jnp.arange(per_group, dtype=jnp.int32)
    source_pos = jnp.arange(layer_count, dtype=jnp.int32)
    causal = source_pos[None, :] <= target_pos[:, None]
    masked = all_features[None] * causal[:, :, None, None].astype(jnp.bfloat16)
    recon_terms = jnp.einsum(
        "slft,slfd->std", masked, dec_weight, preferred_element_type=jnp.float32
    )
    scale = 1.0 / math.sqrt(TOKENS)
    recon_sum = lax.psum_scatter(recon_terms, "feat", scatter_dimension=1, tiled=True)
    errors = recon_sum - targets.astype(jnp.float32)
    scaled_error = (errors * scale).astype(jnp.bfloat16)
    scaled_full = lax.all_gather(scaled_error, "feat", axis=1, tiled=True)
    grad_dec = jnp.einsum(
        "slft,std->slfd", masked, scaled_full, preferred_element_type=jnp.float32
    ).astype(jnp.bfloat16)
    partial_grad = jnp.einsum(
        "slfd,std->slft", dec_weight, scaled_full, preferred_element_type=jnp.float32
    )
    partial_grad = jnp.sum(partial_grad * causal[:, :, None, None].astype(jnp.float32), axis=0)
    feature_grad = lax.psum_scatter(partial_grad, "layer", scatter_dimension=0, tiled=True)
    pre_grad = (active.astype(jnp.float32) * feature_grad).astype(jnp.bfloat16)
    grad_enc = jnp.einsum(
        "sft,std->sfd", pre_grad, source_full, preferred_element_type=jnp.float32
    ).astype(jnp.bfloat16)
    return (errors, grad_dec, grad_enc)


def solution(mesh):
    in_specs = (
        P("layer", "feat", None),
        P("layer", "feat", None),
        P("layer", "feat", None),
        P("layer", None, "feat", None),
        P("layer", "feat", None),
    )
    out_specs = (P("layer", "feat", None), P("layer", None, "feat", None), P("layer", "feat", None))
    return jax.shard_map(
        on_device, mesh=mesh, in_specs=in_specs, out_specs=out_specs, check_vma=False
    )
```

profile of v0, /device:TPU:1, one launch (start us, length us, event | category | flops | bytes accessed | tf_op | source)
XLA Modules:
  0.0 701.5 jit_solution(4639413504859999546)
XLA Ops:
  7.2 0.0 copy-start
  7.2 0.0 all-gather.3.cloned.1.call-start
  7.2 0.7 all-gather.3.cloned.1.call-update
  7.9 0.0 reduce-scatter.3.cloned.1.call-start
  8.0 131.2 %all-gather.3.cloned.1.call-done = bf16[1,512,4096]{2,1,0:T(8,128)(2,1)} async-done(((bf16[1,8,4096]{2,1,0:T(8,128)(2,1)}), bf16[1,512,4096]{2,1,0:T(8,128)(2,1)}) %all-gather.3.cloned.1.call-update) | async-done | bytes 4194320 | tf_op jit(solution)/shard_map/all_gather | solution.py:14
  139.2 0.0 copy-done
  139.2 0.0 copy-start.1
  139.2 3.9 fusion.26
  143.1 10.6 %all_gather.10 = bf16[4,128,512]{2,1,0:T(8,128)(2,1)S(1)} all-gather(bf16[1,128,512]{2,1,0:T(8,128)(2,1)S(1)} %fusion.26), channel_id=1, replica_groups=mesh['layer'=4,'feat'=64] {'layer'}, dimensions={0}, use_global_device_ids=true | all-gather | bytes 655360 | tf_op jit(solution)/shard_map/all_gather | solution.py:19
  153.7 0.0 copy-done.1
  153.7 5.7 convolution_bitcast_fusion
  159.4 0.0 copy-start.3
  159.4 0.0 reduce-scatter.3.cloned.1.call-update
  159.5 0.0 all-gather.5.cloned.1.call-start
  159.5 334.9 %reduce-scatter.3.cloned.1.call-done = f32[1,8,4096]{2,1,0:T(8,128)} async-done(((f32[1,512,4096]{2,1,0:T(8,128)}), f32[1,8,4096]{2,1,0:T(8,128)}) %reduce-scatter.3.cloned.1.call-update) | async-done | bytes 131088 | tf_op jit(solution)/shard_map/reduce_scatter | solution.py:28
  494.4 0.0 copy-done.3
  494.4 1.6 multiply_convert_fusion.1
  496.0 0.0 all-gather.5.cloned.1.call-update
  496.0 0.0 reduce-scatter.5.cloned.1.call-start
  496.1 164.2 %all-gather.5.cloned.1.call-done = bf16[1,512,4096]{2,1,0:T(8,128)(2,1)} async-done(((bf16[1,8,4096]{2,1,0:T(8,128)(2,1)}), bf16[1,512,4096]{2,1,0:T(8,128)(2,1)}) %all-gather.5.cloned.1.call-update) | async-done | bytes 4194320 | tf_op jit(solution)/shard_map/all_gather | solution.py:31
  660.3 6.8 fusion.15
  667.1 0.0 reduce-scatter.5.cloned.1.call-update
  667.1 0.0 copy-start.2
  667.1 6.6 fusion
  673.7 17.2 %reduce-scatter.5.cloned.1.call-done = f32[1,128,512]{2,1,0:T(8,128)} async-done(((f32[4,128,512]{2,1,0:T(8,128)}), f32[1,128,512]{2,1,0:T(8,128)}) %reduce-scatter.5.cloned.1.call-update) | async-done | bytes 262160 | tf_op jit(solution)/shard_map/reduce_scatter | solution.py:39
  691.0 0.0 copy-done.2
  691.0 4.0 fusion.1
  (2 shorter events, 0.0 us)
Async XLA Ops:
  7.2 132.1 %copy-start = (bf16[1,128,4096]{2,1,0:T(8,128)(2,1)S(1)}, bf16[1,128,4096]{2,1,0:T(8,128)(2,1)}, u32[]{:S(2)}) copy-start(bf16[1,128,4096]{2,1,0:T(8,128)(2,1)} %param.7) | copy-start | bytes 3145732
  7.2 132.0 %all-gather.3.cloned.1.call-start = ((), (), s32[]{:S(2)}) async-start(), calls=%async_computation.2 | async-start | bytes 4259840 | tf_op jit(solution)/shard_map/all_gather | solution.py:14
  7.9 486.5 %reduce-scatter.3.cloned.1.call-start = ((), (), s32[]{:S(2)}) async-start(), calls=%async_computation.3 | async-start | bytes 8519680 | tf_op jit(solution)/shard_map/reduce_scatter | solution.py:28
  139.2 14.5 %copy-start.1 = (bf16[1,4,128,4096]{3,2,1,0:T(8,128)(2,1)S(1)}, bf16[1,4,128,4096]{3,2,1,0:T(8,128)(2,1)}, u32[]{:S(2)}) copy-start(bf16[1,4,128,4096]{3,2,1,0:T(8,128)(2,1)} %param.8) | copy-start | bytes 12582916
  159.4 335.0 %copy-start.3 = (bf16[1,8,4096]{2,1,0:T(8,128)(2,1)S(1)}, bf16[1,8,4096]{2,1,0:T(8,128)(2,1)}, u32[]{:S(2)}) copy-start(bf16[1,8,4096]{2,1,0:T(8,128)(2,1)} %param.6) | copy-start | bytes 196612
  159.5 500.8 %all-gather.5.cloned.1.call-start = ((), (), s32[]{:S(2)}) async-start(), calls=%async_computation.4 | async-start | bytes 4259840 | tf_op jit(solution)/shard_map/all_gather | solution.py:31
  496.0 194.9 %reduce-scatter.5.cloned.1.call-start = ((), (), s32[]{:S(2)}) async-start(), calls=%async_computation.5 | async-start | bytes 1310720 | tf_op jit(solution)/shard_map/reduce_scatter | solution.py:39
  667.1 23.9 %copy-start.2 = (s32[1,128,512]{2,1,0:T(8,128)S(1)}, s32[1,128,512]{2,1,0:T(8,128)}, u32[]{:S(2)}) copy-start(s32[1,128,512]{2,1,0:T(8,128)} %param.9) | copy-start | bytes 786436
Sparse Core Ops, SparseCore 0:
  11.5 127.6 all-gather.2
  159.6 334.7 reduce-scatter.2
  498.5 161.7 all-gather.4
  667.2 23.6 reduce-scatter.4
where the time goes:
time: 702 us; the launch traced here: 701 us
  waiting for transfers between devices  648 us (92%)
  matrix products  27 us (4%)
  between operations  13.8 us (2%)
  blocking collectives  10.6 us (2%)
    reduce_scatter x1, waiting for transfers between devices, on_device(): lax.psum_scatter(recon_terms, 'feat', scatter_dimension=1, tiled=True)  335 us
    all_gather x1, waiting for transfers between devices, on_device(): scaled_full = lax.all_gather(scaled_error, 'feat', axis=1, tiled=True)  164 us
    all_gather x1, waiting for transfers between devices, on_device(): source_full = lax.all_gather(sources, 'feat', axis=1, tiled=True)  131 us
    reduce_scatter x1, waiting for transfers between devices, on_device(): lax.psum_scatter(partial_grad, 'layer', scatter_dimension=0, tiled=True)  17.2 us
  transfers between devices with their start and end apart: 4, of which 4 were waited for; matrix products, arithmetic and copies ran while one was open for 1% of the time, Pallas kernels for 0%

commit v1 on v0

--- a/solution.py
+++ b/solution.py
@@ -28,7 +28,8 @@
     recon_sum = lax.psum_scatter(recon_terms, "feat", scatter_dimension=1, tiled=True)
     errors = recon_sum - targets.astype(jnp.float32)
     scaled_error = (errors * scale).astype(jnp.bfloat16)
-    scaled_full = lax.all_gather(scaled_error, "feat", axis=1, tiled=True)
+    sent = jnp.stack([scaled_error] * lax.axis_size("feat"))
+    scaled_full = jnp.concatenate(lax.all_to_all(sent, "feat", 0, 0), axis=1)
     grad_dec = jnp.einsum(
         "slft,std->slfd", masked, scaled_full, preferred_element_type=jnp.float32
     ).astype(jnp.bfloat16)

time: 702 us -> 648 us (0.923)
  waiting for transfers between devices: 648 us -> 587 us
    all_gather x1 -> x0, waiting for transfers between devices: 164 us -> none  [on_device(): scaled_full = lax.all_gather(scaled_error, 'feat', axis=1, tiled=True)]
    reduce_scatter x1, waiting for transfers between devices: 17.2 us -> 69 us  [on_device(): lax.psum_scatter(partial_grad, 'layer', scatter_dimension=0, tiled=True)]
    all_to_all x0 -> x1, waiting for transfers between devices: none -> 51 us  [on_device(): scaled_full = jnp.concatenate(lax.all_to_all(sent, 'feat', 0, 0), axis=1)]
where the time goes in v1:
time: 648 us
  waiting for transfers between devices  587 us (91%)
  matrix products  27 us (4%)
  between operations  13.8 us (2%)
  blocking collectives  10.6 us (2%)
    reduce_scatter x1, waiting for transfers between devices, on_device(): lax.psum_scatter(recon_terms, 'feat', scatter_dimension=1, tiled=True)  335 us
    all_gather x1, waiting for transfers between devices, on_device(): source_full = lax.all_gather(sources, 'feat', axis=1, tiled=True)  131 us
    reduce_scatter x1, waiting for transfers between devices, on_device(): lax.psum_scatter(partial_grad, 'layer', scatter_dimension=0, tiled=True)  69 us
    all_to_all x1, waiting for transfers between devices, on_device(): scaled_full = jnp.concatenate(lax.all_to_all(sent, 'feat', 0, 0), axis=1)  51 us
  transfers between devices with their start and end apart: 4, of which 4 were waited for; matrix products, arithmetic and copies ran while one was open for 1% of the time, Pallas kernels for 0%

profile of v1, /device:TPU:1, one launch (start us, length us, event | category | flops | bytes accessed | tf_op | source)
XLA Modules:
  0.0 648.1 jit_solution(1283506643641131814)
XLA Ops:
  7.2 0.0 copy-start
  7.2 0.0 all-gather.2.cloned.1.call-start
  7.2 0.7 all-gather.2.cloned.1.call-update
  7.9 0.0 reduce-scatter.3.cloned.1.call-start
  8.0 131.2 %all-gather.2.cloned.1.call-done = bf16[1,512,4096]{2,1,0:T(8,128)(2,1)} async-done(((bf16[1,8,4096]{2,1,0:T(8,128)(2,1)}), bf16[1,512,4096]{2,1,0:T(8,128)(2,1)}) %all-gather.2.cloned.1.call-update) | async-done | bytes 4194320 | tf_op jit(solution)/shard_map/all_gather | solution.py:14
  139.2 0.0 copy-done
  139.2 0.0 copy-start.1
  139.2 3.9 fusion.26
  143.1 10.6 %all_gather.7 = bf16[4,128,512]{2,1,0:T(8,128)(2,1)S(1)} all-gather(bf16[1,128,512]{2,1,0:T(8,128)(2,1)S(1)} %fusion.26), channel_id=1, replica_groups=mesh['layer'=4,'feat'=64] {'layer'}, dimensions={0}, use_global_device_ids=true | all-gather | bytes 655360 | tf_op jit(solution)/shard_map/all_gather | solution.py:19
  153.7 0.0 copy-done.1
  153.7 5.7 convolution_bitcast_fusion
  159.4 0.0 copy-start.3
  159.4 0.0 reduce-scatter.3.cloned.1.call-update
  159.5 334.9 %reduce-scatter.3.cloned.1.call-done = f32[1,8,4096]{2,1,0:T(8,128)} async-done(((f32[1,512,4096]{2,1,0:T(8,128)}), f32[1,8,4096]{2,1,0:T(8,128)}) %reduce-scatter.3.cloned.1.call-update) | async-done | bytes 131088 | tf_op jit(solution)/shard_map/reduce_scatter | solution.py:28
  494.4 0.0 copy-done.3
  494.4 1.6 fusion.36
  496.0 2.5 stack.2
  498.5 5.7 all-to-all-start
  504.2 0.0 reduce-scatter.5.cloned.1.call-start
  504.2 51.0 %all-to-all-done = bf16[64,1,8,4096]{3,2,1,0:T(8,128)(2,1)} async-done(((bf16[64,1,8,4096]{3,2,1,0:T(8,128)(2,1)}), bf16[64,1,8,4096]{3,2,1,0:T(8,128)(2,1)}, u32[]{:S(2)}, u32[]{:S(2)}) %all-to-all-start) | async-done | bytes 4194336 | tf_op jit(solution)/shard_map/all_to_all | solution.py:32
  555.2 6.8 %fusion.15 = f32[4,128,512]{2,1,0:T(8,128)} fusion(bf16[1,4,128,4096]{3,2,1,0:T(8,128)(2,1)} %param.8, bf16[64,1,8,4096]{3,2,1,0:T(8,128)(2,1)} %all-to-all-done, f32[4]{0:T(128)S(1)} %compare_convert_fusion), kind=kOutput, calls=%fused_computation.14 | convolution fusion | flops 2147745792 | bytes 9437200 | tf_op jit(solution)/shard_map/slfd,std->slft/dot_general | solution.py:36
  562.0 0.0 reduce-scatter.5.cloned.1.call-update
  562.0 0.0 copy-start.2
  562.1 6.6 %fusion = bf16[1,4,128,4096]{3,2,1,0:T(8,128)(2,1)} fusion(bf16[64,1,8,4096]{3,2,1,0:T(8,128)(2,1)} %all-to-all-done, bf16[4,128,512]{2,1,0:T(8,128)(2,1)S(1)} %all_gather.7, bf16[4]{0:T(256)(128)(2,1)S(1)} %compare_convert_fusion.1), kind=kOutput, calls=%fused_computation.2 | convolution fusion | flops 2149842944 | bytes 8912904 | tf_op jit(solution)/shard_map/slft,std->slfd/dot_general | solution.py:33
  568.7 69.0 %reduce-scatter.5.cloned.1.call-done = f32[1,128,512]{2,1,0:T(8,128)} async-done(((f32[4,128,512]{2,1,0:T(8,128)}), f32[1,128,512]{2,1,0:T(8,128)}) %reduce-scatter.5.cloned.1.call-update) | async-done | bytes 262160 | tf_op jit(solution)/shard_map/reduce_scatter | solution.py:40
  637.6 0.0 copy-done.2
  637.6 4.0 fusion.1
  (2 shorter events, 0.0 us)
Async XLA Ops:
  7.2 132.1 %copy-start = (bf16[1,128,4096]{2,1,0:T(8,128)(2,1)S(1)}, bf16[1,128,4096]{2,1,0:T(8,128)(2,1)}, u32[]{:S(2)}) copy-start(bf16[1,128,4096]{2,1,0:T(8,128)(2,1)} %param.7) | copy-start | bytes 3145732
  7.2 132.0 %all-gather.2.cloned.1.call-start = ((), (), s32[]{:S(2)}) async-start(), calls=%async_computation.3 | async-start | bytes 4259840 | tf_op jit(solution)/shard_map/all_gather | solution.py:14
  7.9 486.5 %reduce-scatter.3.cloned.1.call-start = ((), (), s32[]{:S(2)}) async-start(), calls=%async_computation.4 | async-start | bytes 8519680 | tf_op jit(solution)/shard_map/reduce_scatter | solution.py:28
  139.2 14.5 %copy-start.1 = (bf16[1,4,128,4096]{3,2,1,0:T(8,128)(2,1)S(1)}, bf16[1,4,128,4096]{3,2,1,0:T(8,128)(2,1)}, u32[]{:S(2)}) copy-start(bf16[1,4,128,4096]{3,2,1,0:T(8,128)(2,1)} %param.8) | copy-start | bytes 12582916
  159.4 335.0 %copy-start.3 = (bf16[1,8,4096]{2,1,0:T(8,128)(2,1)S(1)}, bf16[1,8,4096]{2,1,0:T(8,128)(2,1)}, u32[]{:S(2)}) copy-start(bf16[1,8,4096]{2,1,0:T(8,128)(2,1)} %param.6) | copy-start | bytes 196612
  498.5 56.7 %all-to-all-start = ((bf16[64,1,8,4096]{3,2,1,0:T(8,128)(2,1)}), bf16[64,1,8,4096]{3,2,1,0:T(8,128)(2,1)}, u32[]{:S(2)}, u32[]{:S(2)}) async-start(bf16[64,1,8,4096]{3,2,1,0:T(8,128)(2,1)} %stack.2), calls=%async_computation.1 | async-start | bytes 8388608 | tf_op jit(solution)/shard_map/all_to_all | solution.py:32
  504.2 133.5 %reduce-scatter.5.cloned.1.call-start = ((), (), s32[]{:S(2)}) async-start(), calls=%async_computation.5 | async-start | bytes 1310720 | tf_op jit(solution)/shard_map/reduce_scatter | solution.py:40
  562.0 75.6 %copy-start.2 = (s32[1,128,512]{2,1,0:T(8,128)S(1)}, s32[1,128,512]{2,1,0:T(8,128)}, u32[]{:S(2)}) copy-start(s32[1,128,512]{2,1,0:T(8,128)} %param.9) | copy-start | bytes 786436
Sparse Core Ops, SparseCore 0:
  11.5 127.6 all-gather.1
  159.6 334.7 reduce-scatter.2
  562.2 75.4 reduce-scatter.4
